TPU v7x, 32 devices: a whole 2x2x4 slice. The times are simulated.
32 devices in a mesh: dp: 16 (over z, x, core), mp: 2 (over y).
Axes of the slice: x: 2, y: 2, z: 4, core: 2. Of those that a mesh axis runs over, the one named last changes fastest.
Arguments:
- tokens: bfloat16 [64, 512, 768], P('dp', 'mp'), may hold values from -6 to 6
- lengths: int32 [64], P('dp'), may hold values from 128 to 512, as said below
- out_grad: bfloat16 [64, 512, 768], P('dp', 'mp'), may hold values from -6 to 6
- ln1_gain: float32 [768], replicated, may hold values from 0.25 to 1.75
- ln1_shift: float32 [768], replicated, may hold values from -1.75 to 1.75
- w_query: bfloat16 [768, 768], P(None, 'mp'), may hold values from -0.21875 to 0.21875
- b_query: float32 [768], P('mp'), may hold values from -3 to 3
- w_key: bfloat16 [768, 768], P(None, 'mp'), may hold values from -0.21875 to 0.21875
- w_value: bfloat16 [768, 768], P(None, 'mp'), may hold values from -0.21875 to 0.21875
- b_value: float32 [768], P('mp'), may hold values from -3 to 3
- w_out: bfloat16 [768, 768], P('mp'), may hold values from -1.75 to 1.75
- b_out: float32 [768], replicated, may hold values from -1.75 to 1.75
- ln2_gain: float32 [768], replicated, may hold values from 0.25 to 1.75
- ln2_shift: float32 [768], replicated, may hold values from -1.75 to 1.75
- w_up: bfloat16 [768, 3072], P(None, 'mp'), may hold values from -0.21875 to 0.21875
- b_up: float32 [3072], P('mp'), may hold values from -3 to 3
- w_down: bfloat16 [3072, 768], P('mp'), may hold values from -0.109375 to 0.109375
- b_down: float32 [768], replicated, may hold values from -1.75 to 1.75
Outputs:
- block_out: bfloat16 [64, 512, 768], P('dp', 'mp')
- input_grad: float32 [64, 512, 768], P('dp', 'mp')
- grad_ln1_gain: float32 [768], replicated
- grad_ln1_shift: float32 [768], replicated
- grad_w_query: float32 [768, 768], P(None, 'mp')
- grad_b_query: float32 [768], P('mp')
- grad_w_key: float32 [768, 768], P(None, 'mp')
- grad_w_value: float32 [768, 768], P(None, 'mp')
- grad_b_value: float32 [768], P('mp')
- grad_w_out: float32 [768, 768], P('mp')
- grad_b_out: float32 [768], replicated
- grad_ln2_gain: float32 [768], replicated
- grad_ln2_shift: float32 [768], replicated
- grad_w_up: float32 [768, 3072], P(None, 'mp')
- grad_b_up: float32 [3072], P('mp')
- grad_w_down: float32 [3072, 768], P('mp')
- grad_b_down: float32 [768], replicated
Inputs may be any that keep to these rules, and one draw needn't show every extreme that they name: lengths of the rows; some row has 512 and some row a quarter of 512.
All inputs are finite; a program needn't handle non-finite values.
Results may differ from a plain program's by a relative error of at most 0.013.
The roundings to bfloat16 on the way count: a program that leaves them out, or rounds other values in their place, can miss the bound.
Values may be sent and summed in bfloat16 or wider, within the bound.
No kernel may reach another device: no remote copies, remote signals or barrier semaphores. Data moves between devices by JAX's collectives and lax.ppermute only.
A program may use at most 192 MiB of HBM per device.

v0:
```python
import math
import jax
import jax.numpy as jnp
from jax import lax
from jax.sharding import PartitionSpec as P

HEAD_DIM = 64
SEQ = 512
MB = 4
ROWS_MB = 1
epsilon = 1e-12
masked_fill = -1000000000.0


def layer_norm(values, gain_vec, offset):
    average = jnp.mean(values, axis=-1, keepdims=True)
    centred = values - average
    inv_std = lax.rsqrt(jnp.mean(centred * centred, axis=-1, keepdims=True) + epsilon)
    unit_part = centred * inv_std
    return (unit_part * gain_vec + offset, unit_part, inv_std)


def norm_back(upstream, unit_part, inv_std, gain_vec):
    scaled = upstream * gain_vec
    return inv_std * (
        scaled
        - jnp.mean(scaled, axis=-1, keepdims=True)
        - unit_part * jnp.mean(scaled * unit_part, axis=-1, keepdims=True)
    )


def gelu_slope(values):
    normal_cdf = 0.5 * (1.0 + lax.erf(values * (1.0 / math.sqrt(2.0))))
    return normal_cdf + values * jnp.exp(-0.5 * values * values) * (1.0 / math.sqrt(2.0 * math.pi))


def product(pattern, left_side, right_side):
    return jnp.einsum(pattern, left_side, right_side, preferred_element_type=jnp.float32)


def token_sum(values):
    return jnp.sum(values, axis=(0, 1))


def masked_scores(query_low, keys_low, key_valid, score_scale):
    raw_scores = product("bqhd,bkhd->bhqk", query_low, keys_low) * score_scale
    return jnp.where(key_valid, raw_scores, masked_fill)


def on_device(
    tokens,
    lengths,
    out_grad,
    ln1_gain,
    ln1_shift,
    w_query,
    b_query,
    w_key,
    w_value,
    b_value,
    w_out,
    b_out,
    ln2_gain,
    ln2_shift,
    w_up,
    b_up,
    w_down,
    b_down,
):
    heads_here = w_query.shape[1] // HEAD_DIM
    score_scale = 1.0 / math.sqrt(HEAD_DIM)
    positions = jnp.arange(SEQ, dtype=jnp.int32)
    sum_w_query = jnp.zeros(w_query.shape, jnp.float32)
    sum_b_query = jnp.zeros(b_query.shape, jnp.float32)
    sum_w_key = jnp.zeros(w_key.shape, jnp.float32)
    sum_w_value = jnp.zeros(w_value.shape, jnp.float32)
    sum_b_value = jnp.zeros(b_value.shape, jnp.float32)
    sum_w_out = jnp.zeros(w_out.shape, jnp.float32)
    sum_w_up = jnp.zeros(w_up.shape, jnp.float32)
    sum_b_up = jnp.zeros(b_up.shape, jnp.float32)
    sum_w_down = jnp.zeros(w_down.shape, jnp.float32)
    sum_ln1_gain = jnp.zeros(ln1_gain.shape, jnp.float32)
    sum_ln1_shift = jnp.zeros(ln1_shift.shape, jnp.float32)
    sum_ln2_gain = jnp.zeros(ln2_gain.shape, jnp.float32)
    sum_ln2_shift = jnp.zeros(ln2_shift.shape, jnp.float32)
    sum_b_out = jnp.zeros(b_out.shape, jnp.float32)
    sum_b_down = jnp.zeros(b_down.shape, jnp.float32)
    outputs = []
    input_grads = []
    for micro_idx in range(MB):
        row_start = micro_idx * ROWS_MB
        inputs = tokens[row_start : row_start + ROWS_MB].astype(jnp.float32)
        row_lengths = lengths[row_start : row_start + ROWS_MB]
        upstream = out_grad[row_start : row_start + ROWS_MB]
        normed_in, unit_in, inv_in = layer_norm(inputs, ln1_gain, ln1_shift)
        full_in = lax.all_gather(normed_in.astype(jnp.bfloat16), "mp", axis=1, tiled=True)
        rows_mb = full_in.shape[0]
        query_low = (
            (product("bsd,de->bse", full_in, w_query) + b_query)
            .astype(jnp.bfloat16)
            .reshape(rows_mb, SEQ, heads_here, HEAD_DIM)
        )
        keys_low = (
            product("bsd,de->bse", full_in, w_key)
            .astype(jnp.bfloat16)
            .reshape(rows_mb, SEQ, heads_here, HEAD_DIM)
        )
        values_low = (
            (product("bsd,de->bse", full_in, w_value) + b_value)
            .astype(jnp.bfloat16)
            .reshape(rows_mb, SEQ, heads_here, HEAD_DIM)
        )
        key_valid = (positions[None, :] < row_lengths[:, None])[:, None, None, :]
        scores = masked_scores(query_low, keys_low, key_valid, score_scale)
        row_max = jnp.max(scores, axis=-1, keepdims=True)
        log_total = row_max + jnp.log(jnp.sum(jnp.exp(scores - row_max), axis=-1, keepdims=True))
        prob_low = jnp.exp(scores - log_total).astype(jnp.bfloat16)
        mixed_low = (
            product("bhqk,bkhd->bqhd", prob_low, values_low)
            .reshape(rows_mb, SEQ, heads_here * HEAD_DIM)
            .astype(jnp.bfloat16)
        )
        attended = lax.psum_scatter(
            product("bse,ed->bsd", mixed_low, w_out), "mp", scatter_dimension=1, tiled=True
        )
        residual = inputs + attended + b_out
        normed_mid, unit_mid, inv_mid = layer_norm(residual, ln2_gain, ln2_shift)
        full_mid = lax.all_gather(normed_mid.astype(jnp.bfloat16), "mp", axis=1, tiled=True)
        hidden = product("bsd,df->bsf", full_mid, w_up) + b_up
        active = jax.nn.gelu(hidden, approximate=False).astype(jnp.bfloat16)
        branch = lax.psum_scatter(
            product("bsf,fd->bsd", active, w_down).astype(jnp.bfloat16),
            "mp",
            scatter_dimension=1,
            tiled=True,
        ).astype(jnp.float32)
        outputs.append((residual + branch + b_down).astype(jnp.bfloat16))
        grad_full = lax.all_gather(upstream, "mp", axis=1, tiled=True)
        upstream_f = upstream.astype(jnp.float32)
        sum_w_down = sum_w_down + product("bsf,bsd->fd", active, grad_full)
        sum_b_down = sum_b_down + token_sum(upstream_f)
        grad_hidden = (product("bsd,fd->bsf", grad_full, w_down) * gelu_slope(hidden)).astype(
            jnp.bfloat16
        )
        sum_w_up = sum_w_up + product("bsd,bsf->df", full_mid, grad_hidden)
        sum_b_up = sum_b_up + token_sum(grad_hidden.astype(jnp.float32))
        grad_norm_mid = lax.psum_scatter(
            product("bsf,df->bsd", grad_hidden, w_up), "mp", scatter_dimension=1, tiled=True
        )
        sum_ln2_gain = sum_ln2_gain + token_sum(grad_norm_mid * unit_mid)
        sum_ln2_shift = sum_ln2_shift + token_sum(grad_norm_mid)
        grad_residual = upstream_f + norm_back(grad_norm_mid, unit_mid, inv_mid, ln2_gain)
        sum_b_out = sum_b_out + token_sum(grad_residual)
        grad_attn = lax.all_gather(grad_residual.astype(jnp.bfloat16), "mp", axis=1, tiled=True)
        sum_w_out = sum_w_out + product("bse,bsd->ed", mixed_low, grad_attn)
        grad_mixed = (
            product("bsd,ed->bse", grad_attn, w_out)
            .astype(jnp.bfloat16)
            .reshape(rows_mb, SEQ, heads_here, HEAD_DIM)
        )
        grad_probs = product("bqhd,bkhd->bhqk", grad_mixed, values_low)
        probs_full = jnp.exp(masked_scores(query_low, keys_low, key_valid, score_scale) - log_total)
        row_delta = jnp.sum(probs_full * grad_probs, axis=-1, keepdims=True)
        grad_scores = (probs_full * (grad_probs - row_delta)).astype(jnp.bfloat16)
        grad_query = (
            (product("bhqk,bkhd->bqhd", grad_scores, keys_low) * score_scale)
            .astype(jnp.bfloat16)
            .reshape(rows_mb, SEQ, heads_here * HEAD_DIM)
        )
        grad_keys = (
            (product("bhqk,bqhd->bkhd", grad_scores, query_low) * score_scale)
            .astype(jnp.bfloat16)
            .reshape(rows_mb, SEQ, heads_here * HEAD_DIM)
        )
        grad_values = (
            product("bhqk,bqhd->bkhd", prob_low, grad_mixed)
            .astype(jnp.bfloat16)
            .reshape(rows_mb, SEQ, heads_here * HEAD_DIM)
        )
        sum_w_query = sum_w_query + product("bsd,bse->de", full_in, grad_query)
        sum_b_query = sum_b_query + token_sum(grad_query.astype(jnp.float32))
        sum_w_key = sum_w_key + product("bsd,bse->de", full_in, grad_keys)
        sum_w_value = sum_w_value + product("bsd,bse->de", full_in, grad_values)
        sum_b_value = sum_b_value + token_sum(grad_values.astype(jnp.float32))
        input_terms = (
            product("bse,de->bsd", grad_query, w_query)
            + product("bse,de->bsd", grad_keys, w_key)
            + product("bse,de->bsd", grad_values, w_value)
        )
        grad_norm_in = lax.psum_scatter(
            input_terms.astype(jnp.bfloat16), "mp", scatter_dimension=1, tiled=True
        ).astype(jnp.float32)
        sum_ln1_gain = sum_ln1_gain + token_sum(grad_norm_in * unit_in)
        sum_ln1_shift = sum_ln1_shift + token_sum(grad_norm_in)
        input_grads.append(grad_residual + norm_back(grad_norm_in, unit_in, inv_in, ln1_gain))
    totals = tuple(
        lax.psum(
            (
                sum_w_query,
                sum_b_query,
                sum_w_key,
                sum_w_value,
                sum_b_value,
                sum_w_out,
                sum_w_up,
                sum_b_up,
                sum_w_down,
            ),
            "dp",
        )
    )
    common = lax.psum(
        (sum_ln1_gain, sum_ln1_shift, sum_ln2_gain, sum_ln2_shift, sum_b_out, sum_b_down),
        ("dp", "mp"),
    )
    block_out = jnp.concatenate(outputs, axis=0)
    input_grad = jnp.concatenate(input_grads, axis=0)
    return (
        block_out,
        input_grad,
        common[0],
        common[1],
        totals[0],
        totals[1],
        totals[2],
        totals[3],
        totals[4],
        totals[5],
        common[4],
        common[2],
        common[3],
        totals[6],
        totals[7],
        totals[8],
        common[5],
    )


def solution(mesh):
    in_specs = (
        P("dp", "mp", None),
        P("dp"),
        P("dp", "mp", None),
        P(),
        P(),
        P(None, "mp"),
        P("mp"),
        P(None, "mp"),
        P(None, "mp"),
        P("mp"),
        P("mp", None),
        P(),
        P(),
        P(),
        P(None, "mp"),
        P("mp"),
        P("mp", None),
        P(),
    )
    out_specs = (
        P("dp", "mp", None),
        P("dp", "mp", None),
        P(),
        P(),
        P(None, "mp"),
        P("mp"),
        P(None, "mp"),
        P(None, "mp"),
        P("mp"),
        P("mp", None),
        P(),
        P(),
        P(),
        P(None, "mp"),
        P("mp"),
        P("mp", None),
        P(),
    )
    return jax.shard_map(
        on_device, mesh=mesh, in_specs=in_specs, out_specs=out_specs, check_vma=False
    )
```

profile of v0, /device:TPU:0, one launch (start us, length us, event | category | flops | bytes accessed | tf_op | source)
XLA Modules:
  0.0 932.4 jit_solution(8912068039627414131)
XLA Ops:
  12.2 12.8 %all_gather.52 = bf16[1,512,768]{2,1,0:T(8,128)(2,1)S(1)} all-gather(bf16[1,256,768]{2,1,0:T(8,128)(2,1)S(1)} %fusion.127), channel_id=1, replica_groups=mesh['dp'=16,'mp'=2] {'mp'}, dimensions={1}, use_global_device_ids=true | all-gather | bytes 1179648 | tf_op jit(solution)/shard_map/all_gather | solution.py:96
  38.1 2.4 fusion.226
  40.5 16.8 %all_gather.60 = bf16[1,512,768]{2,1,0:T(8,128)(2,1)} all-gather(bf16[1,256,768]{2,1,0:T(8,128)(2,1)S(1)} %get-tuple-element.113), channel_id=1, replica_groups=mesh['dp'=16,'mp'=2] {'mp'}, dimensions={1}, use_global_device_ids=true | all-gather | bytes 1179648 | tf_op jit(solution)/shard_map/all_gather | solution.py:138
  57.3 12.3 %reduce-scatter.25.cloned.1.call-done = f32[1,256,768]{2,1,0:T(8,128)} async-done(((f32[1,512,768]{2,1,0:T(8,128)}), f32[1,256,768]{2,1,0:T(8,128)}) %reduce-scatter.25.cloned.1.call-update) | async-done | bytes 786448 | tf_op jit(solution)/shard_map/reduce_scatter | solution.py:123
  72.2 12.0 %all_gather.53 = bf16[1,512,768]{2,1,0:T(8,128)(2,1)S(1)} all-gather(bf16[1,256,768]{2,1,0:T(8,128)(2,1)S(1)} %add_convert_fusion.7), channel_id=1, replica_groups=mesh['dp'=16,'mp'=2] {'mp'}, dimensions={1}, use_global_device_ids=true | all-gather | bytes 1179648 | tf_op jit(solution)/shard_map/all_gather | solution.py:128
  84.2 10.3 %fusion.16 = (bf16[512,1536]{1,0:T(8,128)(2,1)}, f32[512,1536]{1,0:T(8,128)S(1)}) fusion(f32[1536]{0:T(1024)} %param.33, bf16[768,1536]{1,0:T(8,128)(2,1)S(1)} %copy-done, bf16[1,512,768]{2,1,0:T(8,128)(2,1)S(1)} %all_gather.53), kind=kOutput, calls=%fused_computation.54 | convolution fusion | flops 1259864064 | bytes 7870464 | tf_op jit(solution)/shard_map/bsd,df->bsf/dot_general | solution.py:38
  94.5 2.8 convert_reduce_fusion.1
  98.5 2.6 convolution_bitcast_fusion.5
  101.2 4.4 fusion.70
  105.7 22.8 %reduce-scatter.41.cloned.1.call-done = f32[1,256,768]{2,1,0:T(8,128)} async-done(((f32[1,512,768]{2,1,0:T(8,128)}), f32[1,256,768]{2,1,0:T(8,128)}) %reduce-scatter.41.cloned.1.call-update) | async-done | bytes 786448 | tf_op jit(solution)/shard_map/reduce_scatter | solution.py:147
  131.2 17.6 %reduce-scatter.27.cloned.1.call-done = bf16[1,256,768]{2,1,0:T(8,128)(2,1)} async-done(((bf16[1,512,768]{2,1,0:T(8,128)(2,1)}), bf16[1,256,768]{2,1,0:T(8,128)(2,1)}) %reduce-scatter.27.cloned.1.call-update) | async-done | bytes 393232 | tf_op jit(solution)/shard_map/reduce_scatter | solution.py:131
  148.8 3.6 convert_reduce_fusion.14
  152.5 12.1 %all_gather.61 = bf16[1,512,768]{2,1,0:T(8,128)(2,1)S(1)} all-gather(bf16[1,256,768]{2,1,0:T(8,128)(2,1)S(1)} %convert_element_type.620), channel_id=1, replica_groups=mesh['dp'=16,'mp'=2] {'mp'}, dimensions={1}, use_global_device_ids=true | all-gather | bytes 1179648 | tf_op jit(solution)/shard_map/all_gather | solution.py:154
  165.5 4.5 multiply_reduce_fusion.1
  181.2 15.7 %reduce-scatter.43.cloned.1.call-done = bf16[1,256,768]{2,1,0:T(8,128)(2,1)} async-done(((bf16[1,512,768]{2,1,0:T(8,128)(2,1)}), bf16[1,256,768]{2,1,0:T(8,128)(2,1)}) %reduce-scatter.43.cloned.1.call-update) | async-done | bytes 393232 | tf_op jit(solution)/shard_map/reduce_scatter | solution.py:190
  196.9 3.0 fusion.154
  199.9 2.6 fusion.139
  202.5 11.8 %all_gather.54 = bf16[1,512,768]{2,1,0:T(8,128)(2,1)S(1)} all-gather(bf16[1,256,768]{2,1,0:T(8,128)(2,1)S(1)} %get-tuple-element.97), channel_id=1, replica_groups=mesh['dp'=16,'mp'=2] {'mp'}, dimensions={1}, use_global_device_ids=true | all-gather | bytes 1179648 | tf_op jit(solution)/shard_map/all_gather | solution.py:96
  228.0 16.7 %all_gather.50 = bf16[1,512,768]{2,1,0:T(8,128)(2,1)S(1)} all-gather(bf16[1,256,768]{2,1,0:T(8,128)(2,1)} %get-tuple-element.96), channel_id=1, replica_groups=mesh['dp'=16,'mp'=2] {'mp'}, dimensions={1}, use_global_device_ids=true | all-gather | bytes 1179648 | tf_op jit(solution)/shard_map/all_gather | solution.py:96
  259.6 9.8 %all_gather.48 = bf16[1,512,768]{2,1,0:T(8,128)(2,1)S(1)} all-gather(bf16[1,256,768]{2,1,0:T(8,128)(2,1)} %get-tuple-element.95), channel_id=1, replica_groups=mesh['dp'=16,'mp'=2] {'mp'}, dimensions={1}, use_global_device_ids=true | all-gather | bytes 1179648 | tf_op jit(solution)/shard_map/all_gather | solution.py:96
  283.6 10.3 %all_gather.62 = bf16[1,512,768]{2,1,0:T(8,128)(2,1)} all-gather(bf16[1,256,768]{2,1,0:T(8,128)(2,1)} %get-tuple-element.112), channel_id=1, replica_groups=mesh['dp'=16,'mp'=2] {'mp'}, dimensions={1}, use_global_device_ids=true | all-gather | bytes 1179648 | tf_op jit(solution)/shard_map/all_gather | solution.py:138
  293.9 17.9 %all_gather.58 = bf16[1,512,768]{2,1,0:T(8,128)(2,1)} all-gather(bf16[1,256,768]{2,1,0:T(8,128)(2,1)} %get-tuple-element.111), channel_id=1, replica_groups=mesh['dp'=16,'mp'=2] {'mp'}, dimensions={1}, use_global_device_ids=true | all-gather | bytes 1179648 | tf_op jit(solution)/shard_map/all_gather | solution.py:138
  311.8 16.6 %all_gather.56 = bf16[1,512,768]{2,1,0:T(8,128)(2,1)} all-gather(bf16[1,256,768]{2,1,0:T(8,128)(2,1)S(1)} %copy-done.115), channel_id=1, replica_groups=mesh['dp'=16,'mp'=2] {'mp'}, dimensions={1}, use_global_device_ids=true | all-gather | bytes 1179648 | tf_op jit(solution)/shard_map/all_gather | solution.py:138
  332.8 11.8 %all_gather.55 = bf16[1,512,768]{2,1,0:T(8,128)(2,1)} all-gather(bf16[1,256,768]{2,1,0:T(8,128)(2,1)S(1)} %get-tuple-element.120), channel_id=1, replica_groups=mesh['dp'=16,'mp'=2] {'mp'}, dimensions={1}, use_global_device_ids=true | all-gather | bytes 1179648 | tf_op jit(solution)/shard_map/all_gather | solution.py:128
  344.7 10.9 %all_gather.51 = bf16[1,512,768]{2,1,0:T(8,128)(2,1)S(1)} all-gather(bf16[1,256,768]{2,1,0:T(8,128)(2,1)S(1)} %get-tuple-element.119), channel_id=1, replica_groups=mesh['dp'=16,'mp'=2] {'mp'}, dimensions={1}, use_global_device_ids=true | all-gather | bytes 1179648 | tf_op jit(solution)/shard_map/all_gather | solution.py:128
  355.6 9.4 %fusion.13 = (bf16[512,1536]{1,0:T(8,128)(2,1)}, f32[512,1536]{1,0:T(8,128)S(1)}) fusion(f32[1536]{0:T(1024)S(1)} %copy-done.189, bf16[768,1536]{1,0:T(8,128)(2,1)S(1)} %copy-done, bf16[1,512,768]{2,1,0:T(8,128)(2,1)S(1)} %all_gather.51), kind=kOutput, calls=%fused_computation.51 | convolution fusion | flops 1259864064 | bytes 7870464 | tf_op jit(solution)/shard_map/bsd,df->bsf/dot_general | solution.py:38
  365.0 10.5 %all_gather.49 = bf16[1,512,768]{2,1,0:T(8,128)(2,1)} all-gather(bf16[1,256,768]{2,1,0:T(8,128)(2,1)S(1)} %get-tuple-element.118), channel_id=1, replica_groups=mesh['dp'=16,'mp'=2] {'mp'}, dimensions={1}, use_global_device_ids=true | all-gather | bytes 1179648 | tf_op jit(solution)/shard_map/all_gather | solution.py:128
  375.5 2.8 convert_reduce_fusion.2
  379.5 2.5 convolution_bitcast_fusion.6
  382.2 9.8 %fusion.19 = (bf16[512,1536]{1,0:T(8,128)(2,1)}, f32[512,1536]{1,0:T(8,128)S(1)}) fusion(f32[1536]{0:T(1024)S(1)} %copy-done.189, bf16[768,1536]{1,0:T(8,128)(2,1)S(1)} %copy-done, bf16[1,512,768]{2,1,0:T(8,128)(2,1)} %all_gather.55), kind=kOutput, calls=%fused_computation.57 | convolution fusion | flops 1259864064 | bytes 7870464 | tf_op jit(solution)/shard_map/bsd,df->bsf/dot_general | solution.py:38
  392.0 2.8 convert_reduce_fusion
  396.0 2.6 convolution_bitcast_fusion.4
  398.9 9.8 %fusion.10 = (bf16[512,1536]{1,0:T(8,128)(2,1)}, f32[512,1536]{1,0:T(8,128)S(1)}) fusion(f32[1536]{0:T(1024)S(1)} %copy-done.189, bf16[768,1536]{1,0:T(8,128)(2,1)S(1)} %copy-done, bf16[1,512,768]{2,1,0:T(8,128)(2,1)} %all_gather.49), kind=kOutput, calls=%fused_computation.48 | convolution fusion | flops 1259864064 | bytes 7870464 | tf_op jit(solution)/shard_map/bsd,df->bsf/dot_general | solution.py:38
  408.7 2.8 convert_reduce_fusion.3
  412.7 2.6 convolution_bitcast_fusion.7
  415.4 4.5 fusion.68
  420.0 5.4 fusion.162
  425.4 3.6 fusion.184
  429.1 3.5 fusion.173
  435.2 5.4 fusion.193
  440.6 3.6 fusion.202
  444.2 3.6 fusion.167
  450.2 9.8 %add_add_fusion = f32[1536,768]{1,0:T(8,128)} fusion(f32[1536,768]{1,0:T(8,128)} %fusion.162, f32[1536,768]{1,0:T(8,128)} %fusion.173, f32[1536,768]{1,0:T(8,128)} %fusion.167, bf16[512,1536]{1,0:T(8,128)(2,1)} %get-tuple-element.145, bf16[1,512,768]{2,1,0:T(8,128)(2,1)} %all_gather.62), kind=kOutput, calls=%fused_computation.32 | convolution fusion | flops 1211498496 | bytes 21233664 | tf_op jit(solution)/shard_map/bsf,bsd->fd/dot_general | solution.py:38
  460.0 9.1 add_add_fusion.1
  469.1 3.7 multiply_reduce_fusion.7
  472.8 13.2 %reduce-scatter.19.cloned.1.call-done = bf16[1,256,768]{2,1,0:T(8,128)(2,1)} async-done(((bf16[1,512,768]{2,1,0:T(8,128)(2,1)}), bf16[1,256,768]{2,1,0:T(8,128)(2,1)}) %reduce-scatter.19.cloned.1.call-update) | async-done | bytes 393232 | tf_op jit(solution)/shard_map/reduce_scatter | solution.py:131
  486.1 20.2 %reduce-scatter.31.cloned.1.call-done = bf16[1,256,768]{2,1,0:T(8,128)(2,1)} async-done(((bf16[1,512,768]{2,1,0:T(8,128)(2,1)}), bf16[1,256,768]{2,1,0:T(8,128)(2,1)}) %reduce-scatter.31.cloned.1.call-update) | async-done | bytes 393232 | tf_op jit(solution)/shard_map/reduce_scatter | solution.py:131
  506.3 4.9 fusion.215
  511.3 19.5 %all_gather.57 = bf16[1,512,768]{2,1,0:T(8,128)(2,1)S(1)} all-gather(bf16[1,256,768]{2,1,0:T(8,128)(2,1)S(1)} %convert_element_type.586), channel_id=1, replica_groups=mesh['dp'=16,'mp'=2] {'mp'}, dimensions={1}, use_global_device_ids=true | all-gather | bytes 1179648 | tf_op jit(solution)/shard_map/all_gather | solution.py:154
  531.3 2.4 convert_reduce_fusion.19
  544.6 3.2 fusion.214
  547.8 8.5 all_gather.59
  557.2 4.6 multiply_reduce_fusion.2
  568.1 8.6 all_gather.63
  592.2 3.0 fusion.235
  604.1 2.6 convolution_add_fusion.5
  609.5 3.7 fusion.75
  614.9 2.8 convolution_add_fusion.4
  642.5 60.4 %all-reduce.1 = (f32[384]{0:T(512)}, f32[384]{0:T(512)}, f32[1536]{0:T(1024)}) all-reduce(f32[384]{0:T(512)} %add.700, f32[384]{0:T(512)} %add.710, f32[1536]{0:T(1024)S(1)} %add_add_fusion.2), channel_id=1, replica_groups=mesh['dp'=16,'mp'=2] {'dp'}, use_global_device_ids=true, to_apply=%region_75.76 | all-reduce | flops 2304 | bytes 18432 | tf_op jit(solution)/shard_map/psum | solution.py:197
  707.3 3.6 fusion.155
  713.4 39.4 %all-reduce = (f32[768]{0:T(1024)}, f32[768]{0:T(1024)}, f32[768]{0:T(1024)}, f32[768]{0:T(1024)}, f32[768]{0:T(1024)}, /*index=5*/f32[768]{0:T(1024)}) all-reduce(f32[768]{0:T(1024)} %add_add_fusion.10, f32[768]{0:T(1024)} %add_add_fusion.9, f32[768]{0:T(1024)} %add_add_fusion.6, ...), channel_id=1, replica_groups=mesh['dp'=16,'mp'=2] {'dp','mp'}, use_global_device_ids=true, to_apply=%region_64.65 | all-reduce | flops 4608 | bytes 36864 | tf_op jit(solution)/shard_map/psum | solution.py:212
  756.9 2.9 fusion.142
  763.1 151.8 %all-reduce.5.cloned.1.call-done = (f32[768,384]{1,0:T(8,128)}, f32[768,384]{1,0:T(8,128)}, f32[768,384]{1,0:T(8,128)}, f32[384,768]{1,0:T(8,128)}, f32[768,1536]{1,0:T(8,128)}, /*index=5*/f32[1536,768]{1,0:T(8,128)}) async-done(((f32[768,384]{1,0:T(8,128)}, f32[768,384]{1,0:T(8,128)}, f32[768,384]{1,0:T(8,128)}, f32[384,768]{1,0:T(8,128)}, f32[768,1536]{1,0:T(8,128)}, /*index=5*/f32[1536,768]{1,0:T(8,128)}), ...) | async-done | bytes 14155792 | tf_op jit(solution)/shard_map/psum | solution.py:197
  914.9 2.5 copy.73
  (614 shorter events, 185.8 us)
Async XLA Ops:
  7.2 77.0 %copy-start = (bf16[768,1536]{1,0:T(8,128)(2,1)S(1)}, bf16[768,1536]{1,0:T(8,128)(2,1)}, u32[]{:S(2)}) copy-start(bf16[768,1536]{1,0:T(8,128)(2,1)} %param.32) | copy-start | bytes 7077892
  7.2 17.7 %copy-start.181 = (s32[4]{0:T(128)S(1)}, s32[4]{0:T(128)}, u32[]{:S(2)}) copy-start(s32[4]{0:T(128)} %param.19) | copy-start | bytes 52
  7.2 19.1 %copy-start.35 = (bf16[768,384]{1,0:T(8,128)(2,1)S(1)}, bf16[768,384]{1,0:T(8,128)(2,1)}, u32[]{:S(2)}) copy-start(bf16[768,384]{1,0:T(8,128)(2,1)} %param.25) | copy-start | bytes 1769476
  7.2 19.7 %copy-start.38 = (bf16[768,384]{1,0:T(8,128)(2,1)S(1)}, bf16[768,384]{1,0:T(8,128)(2,1)}, u32[]{:S(2)}) copy-start(bf16[768,384]{1,0:T(8,128)(2,1)} %param.23) | copy-start | bytes 1769476
  7.2 19.7 %copy-start.190 = (f32[384]{0:T(512)S(1)}, f32[384]{0:T(512)}, u32[]{:S(2)}) copy-start(f32[384]{0:T(512)} %param.24) | copy-start | bytes 4612
  7.2 62.3 %reduce-scatter.25.cloned.1.call-start = ((), (), s32[]{:S(2)}) async-start(), calls=%async_computation.20 | async-start | bytes 2359296 | tf_op jit(solution)/shard_map/reduce_scatter | solution.py:123
  8.6 18.9 %copy-start.149 = (f32[256]{0:T(256)}, f32[256]{0:T(256)S(1)}, u32[]{:S(2)}) copy-start(f32[256]{0:T(256)S(1)} %broadcast_multiply_fusion.19) | copy-start | bytes 3076
  10.9 18.2 %copy-start.168 = (f32[256]{0:T(256)}, f32[256]{0:T(256)S(1)}, u32[]{:S(2)}) copy-start(f32[256]{0:T(256)S(1)} %add_rsqrt_fusion.3) | copy-start | bytes 3076
  38.0 90.5 %reduce-scatter.41.cloned.1.call-start = ((), (), s32[]{:S(2)}) async-start(), calls=%async_computation.28 | async-start | bytes 2359296 | tf_op jit(solution)/shard_map/reduce_scatter | solution.py:147
  101.1 47.7 %reduce-scatter.27.cloned.1.call-start = ((), (), s32[]{:S(2)}) async-start(), calls=%async_computation.21 | async-start | bytes 1179648 | tf_op jit(solution)/shard_map/reduce_scatter | solution.py:131
  105.6 91.3 %reduce-scatter.43.cloned.1.call-start = ((), (), s32[]{:S(2)}) async-start(), calls=%async_computation.29 | async-start | bytes 1179648 | tf_op jit(solution)/shard_map/reduce_scatter | solution.py:190
  148.8 15.7 %copy-start.31 = (bf16[384,768]{1,0:T(8,128)(2,1)S(1)}, bf16[384,768]{1,0:T(8,128)(2,1)}, u32[]{:S(2)}) copy-start(bf16[384,768]{1,0:T(8,128)(2,1)} %param.28) | copy-start | bytes 1769476
  152.4 13.0 %copy-start.180 = (pred[512]{0:T(512)(128)(4,1)S(1)}, pred[512]{0:T(512)(128)(4,1)}, u32[]{:S(2)}) copy-start(pred[512]{0:T(512)(128)(4,1)} %copy-done.179) | copy-start | bytes 1540
  177.8 19.2 %copy-start.140 = (f32[768]{0:T(1024)S(1)}, f32[768]{0:T(1024)}, u32[]{:S(2)}) copy-start(f32[768]{0:T(1024)} %param.21) | copy-start | bytes 9220
  179.3 149.1 %reduce-scatter.29.cloned.1.call-start = ((), (), s32[]{:S(2)}) async-start(), calls=%async_computation.22 | async-start | bytes 2359296 | tf_op jit(solution)/shard_map/reduce_scatter | solution.py:123
  180.5 35.0 %copy-start.144 = (f32[256]{0:T(256)}, f32[256]{0:T(256)S(1)}, u32[]{:S(2)}) copy-start(f32[256]{0:T(256)S(1)} %broadcast_multiply_fusion.17) | copy-start | bytes 3076
  181.2 34.4 %copy-start.147 = (f32[256]{0:T(256)}, f32[256]{0:T(256)S(1)}, u32[]{:S(2)}) copy-start(f32[256]{0:T(256)S(1)} %get-tuple-element.181) | copy-start | bytes 3076
  181.2 34.4 %copy-start.148 = (f32[256]{0:T(256)}, f32[256]{0:T(256)S(1)}, u32[]{:S(2)}) copy-start(f32[256]{0:T(256)S(1)} %get-tuple-element.182) | copy-start | bytes 3076
  196.9 17.4 %copy-start.40 = (bf16[768,384]{1,0:T(8,128)(2,1)S(1)}, bf16[768,384]{1,0:T(8,128)(2,1)}, u32[]{:S(2)}) copy-start(bf16[768,384]{1,0:T(8,128)(2,1)} %param.23) | copy-start | bytes 1769476
  199.9 16.2 %copy-start.169 = (f32[256]{0:T(256)}, f32[256]{0:T(256)S(1)}, u32[]{:S(2)}) copy-start(f32[256]{0:T(256)S(1)} %add_rsqrt_fusion.1) | copy-start | bytes 3076
  199.9 16.2 %copy-start.170 = (f32[256]{0:T(256)}, f32[256]{0:T(256)S(1)}, u32[]{:S(2)}) copy-start(f32[256]{0:T(256)S(1)} %add_rsqrt_fusion.5) | copy-start | bytes 3076
  199.9 16.2 %copy-start.171 = (f32[256]{0:T(256)}, f32[256]{0:T(256)S(1)}, u32[]{:S(2)}) copy-start(f32[256]{0:T(256)S(1)} %add_rsqrt_fusion.7) | copy-start | bytes 3076
  202.5 13.6 %copy-start.193 = (f32[384]{0:T(512)S(1)}, f32[384]{0:T(512)}, u32[]{:S(2)}) copy-start(f32[384]{0:T(512)} %param.27) | copy-start | bytes 4612
  225.5 21.2 %copy-start.191 = (f32[384]{0:T(512)S(1)}, f32[384]{0:T(512)}, u32[]{:S(2)}) copy-start(f32[384]{0:T(512)} %param.24) | copy-start | bytes 4612
  227.3 101.2 %reduce-scatter.21.cloned.1.call-start = ((), (), s32[]{:S(2)}) async-start(), calls=%async_computation.18 | async-start | bytes 2359296 | tf_op jit(solution)/shard_map/reduce_scatter | solution.py:123
  228.0 24.0 %copy-start.175 = (pred[512]{0:T(512)(128)(4,1)}, pred[512]{0:T(512)(128)(4,1)S(1)}, u32[]{:S(2)}) copy-start(pred[512]{0:T(512)(128)(4,1)S(1)} %iota_compare_fusion.2) | copy-start | bytes 1540
  258.8 70.4 %reduce-scatter.17.cloned.1.call-start = ((), (), s32[]{:S(2)}) async-start(), calls=%async_computation.16 | async-start | bytes 2359296 | tf_op jit(solution)/shard_map/reduce_scatter | solution.py:123
  259.6 17.0 %copy-start.177 = (pred[512]{0:T(512)(128)(4,1)}, pred[512]{0:T(512)(128)(4,1)S(1)}, u32[]{:S(2)}) copy-start(pred[512]{0:T(512)(128)(4,1)S(1)} %iota_compare_fusion.3) | copy-start | bytes 1540
  281.7 30.1 %copy-start.115 = (bf16[1,256,768]{2,1,0:T(8,128)(2,1)S(1)}, bf16[1,256,768]{2,1,0:T(8,128)(2,1)}, u32[]{:S(2)}) copy-start(bf16[1,256,768]{2,1,0:T(8,128)(2,1)} %get-tuple-element.110) | copy-start | bytes 1179652
  283.5 45.7 %copy-start.166 = (f32[768]{0:T(1024)S(1)}, f32[768]{0:T(1024)}, u32[]{:S(2)}) copy-start(f32[768]{0:T(1024)} %param.29) | copy-start | bytes 9220
  283.5 185.6 %reduce-scatter.37.cloned.1.call-start = ((), (), s32[]{:S(2)}) async-start(), calls=%async_computation.26 | async-start | bytes 2359296 | tf_op jit(solution)/shard_map/reduce_scatter | solution.py:147
  331.6 13.1 %copy-start.14 = (f32[1,256,768]{2,1,0:T(8,128)}, f32[1,256,768]{2,1,0:T(8,128)S(1)}, u32[]{:S(2)}) copy-start(f32[1,256,768]{2,1,0:T(8,128)S(1)} %get-tuple-element.88) | copy-start | bytes 2359300
  331.6 13.1 %copy-start.15 = (f32[1,256,768]{2,1,0:T(8,128)}, f32[1,256,768]{2,1,0:T(8,128)S(1)}, u32[]{:S(2)}) copy-start(f32[1,256,768]{2,1,0:T(8,128)S(1)} %get-tuple-element.107) | copy-start | bytes 2359300
  331.8 137.2 %copy-start.146 = (f32[256]{0:T(256)}, f32[256]{0:T(256)S(1)}, u32[]{:S(2)}) copy-start(f32[256]{0:T(256)S(1)} %broadcast_multiply_fusion.20) | copy-start | bytes 3076
  332.1 137.0 %copy-start.172 = (f32[256]{0:T(256)}, f32[256]{0:T(256)S(1)}, u32[]{:S(2)}) copy-start(f32[256]{0:T(256)S(1)} %add_rsqrt_fusion.4) | copy-start | bytes 3076
  332.3 23.2 %copy-start.189 = (f32[1536]{0:T(1024)S(1)}, f32[1536]{0:T(1024)}, u32[]{:S(2)}) copy-start(f32[1536]{0:T(1024)} %param.33) | copy-start | bytes 18436
  355.6 20.0 %copy-start.85 = (bf16[1,512,768]{2,1,0:T(8,128)(2,1)S(1)}, bf16[1,512,768]{2,1,0:T(8,128)(2,1)}, u32[]{:S(2)}) copy-start(bf16[1,512,768]{2,1,0:T(8,128)(2,1)} %all_gather.58) | copy-start | bytes 2359300
  355.6 20.0 %copy-start.184 = (bf16[1536,768]{1,0:T(8,128)(2,1)S(1)}, bf16[1536,768]{1,0:T(8,128)(2,1)}, u32[]{:S(2)}) copy-start(bf16[1536,768]{1,0:T(8,128)(2,1)} %param.34) | copy-start | bytes 7077892
  382.1 87.0 %reduce-scatter.45.cloned.1.call-start = ((), (), s32[]{:S(2)}) async-start(), calls=%async_computation.30 | async-start | bytes 2359296 | tf_op jit(solution)/shard_map/reduce_scatter | solution.py:147
  398.6 70.4 %reduce-scatter.33.cloned.1.call-start = ((), (), s32[]{:S(2)}) async-start(), calls=%async_computation.24 | async-start | bytes 2359296 | tf_op jit(solution)/shard_map/reduce_scatter | solution.py:147
  415.3 70.8 %reduce-scatter.19.cloned.1.call-start = ((), (), s32[]{:S(2)}) async-start(), calls=%async_computation.17 | async-start | bytes 1179648 | tf_op jit(solution)/shard_map/reduce_scatter | solution.py:131
  419.9 86.4 %reduce-scatter.31.cloned.1.call-start = ((), (), s32[]{:S(2)}) async-start(), calls=%async_computation.23 | async-start | bytes 1179648 | tf_op jit(solution)/shard_map/reduce_scatter | solution.py:131
  434.9 109.7 %reduce-scatter.23.cloned.1.call-start = ((), (), s32[]{:S(2)}) async-start(), calls=%async_computation.19 | async-start | bytes 1179648 | tf_op jit(solution)/shard_map/reduce_scatter | solution.py:131
  450.2 257.0 %reduce-scatter.35.cloned.1.call-start = ((), (), s32[]{:S(2)}) async-start(), calls=%async_computation.25 | async-start | bytes 1179648 | tf_op jit(solution)/shard_map/reduce_scatter | solution.py:190
  469.1 37.2 %copy-start.142 = (f32[768]{0:T(1024)S(1)}, f32[768]{0:T(1024)}, u32[]{:S(2)}) copy-start(f32[768]{0:T(1024)} %param.35) | copy-start | bytes 9220
  506.3 24.5 %copy-start.33 = (bf16[384,768]{1,0:T(8,128)(2,1)S(1)}, bf16[384,768]{1,0:T(8,128)(2,1)}, u32[]{:S(2)}) copy-start(bf16[384,768]{1,0:T(8,128)(2,1)} %param.28) | copy-start | bytes 1769476
  506.3 27.4 %slice-start.4 = ((s8[6291456]{0:T(1024)(128)(4,1)}), s8[4194304]{0:T(1024)(128)(4,1)S(1)}, s32[]{:S(2)}) async-start(s8[6291456]{0:T(1024)(128)(4,1)} %bitcast.416), calls=%async_computation.37 | async-start | bytes 8388608
  511.2 22.5 %copy-start.48 = (f32[1,256,768]{2,1,0:T(8,128)}, f32[1,256,768]{2,1,0:T(8,128)S(1)}, u32[]{:S(2)}) copy-start(f32[1,256,768]{2,1,0:T(8,128)S(1)} %get-tuple-element.82) | copy-start | bytes 2359300
  511.2 20.0 %copy-start.11 = (bf16[6,512,512]{1,2,0:T(8,128)(2,1)S(1)}, bf16[6,512,512]{1,2,0:T(8,128)(2,1)}, u32[]{:S(2)}) copy-start(bf16[6,512,512]{1,2,0:T(8,128)(2,1)} %copy-done.10) | copy-start | bytes 9437188
  511.2 22.5 %slice-start.5 = ((s8[6291456]{0:T(1024)(128)(4,1)}), s8[2097152]{0:T(1024)(128)(4,1)S(1)}, s32[]{:S(2)}) async-start(s8[6291456]{0:T(1024)(128)(4,1)} %bitcast.416), calls=%async_computation.38 | async-start | bytes 4194304
  544.6 12.6 %copy-start.138 = (f32[6,512]{1,0:T(8,128)S(1)}, f32[6,512]{1,0:T(8,128)}, u32[]{:S(2)}) copy-start(f32[6,512]{1,0:T(8,128)} %copy-done.137) | copy-start | bytes 36868
  547.8 14.0 %copy-start.45 = (f32[1,256,768]{2,1,0:T(8,128)}, f32[1,256,768]{2,1,0:T(8,128)S(1)}, u32[]{:S(2)}) copy-start(f32[1,256,768]{2,1,0:T(8,128)S(1)} %get-tuple-element.80) | copy-start | bytes 2359300
  564.2 13.4 %slice-start = ((s8[6291456]{0:T(1024)(128)(4,1)}), s8[4194304]{0:T(1024)(128)(4,1)S(1)}, s32[]{:S(2)}) async-start(s8[6291456]{0:T(1024)(128)(4,1)} %bitcast.412), calls=%async_computation.33 | async-start | bytes 8388608
  588.7 118.5 %reduce-scatter.39.cloned.1.call-start = ((), (), s32[]{:S(2)}) async-start(), calls=%async_computation.27 | async-start | bytes 1179648 | tf_op jit(solution)/shard_map/reduce_scatter | solution.py:190
  609.2 98.0 %reduce-scatter.47.cloned.1.call-start = ((), (), s32[]{:S(2)}) async-start(), calls=%async_computation.31 | async-start | bytes 1179648 | tf_op jit(solution)/shard_map/reduce_scatter | solution.py:190
  623.6 291.2 %all-reduce.5.cloned.1.call-start = ((), (), s32[]{:S(2)}) async-start(), calls=%async_computation.32 | async-start | bytes 28311552 | tf_op jit(solution)/shard_map/psum | solution.py:197
  632.0 71.0 %copy-start.105 = (bf16[1,256,768]{2,1,0:T(8,128)(2,1)S(1)}, bf16[1,256,768]{2,1,0:T(8,128)(2,1)}, u32[]{:S(2)}) copy-start(bf16[1,256,768]{2,1,0:T(8,128)(2,1)} %get-tuple-element.114) | copy-start | bytes 1179652
  632.0 71.0 %copy-start.112 = (bf16[1,256,768]{2,1,0:T(8,128)(2,1)S(1)}, bf16[1,256,768]{2,1,0:T(8,128)(2,1)}, u32[]{:S(2)}) copy-start(bf16[1,256,768]{2,1,0:T(8,128)(2,1)} %get-tuple-element.117) | copy-start | bytes 1179652
  632.0 71.0 %copy-start.116 = (bf16[1,256,768]{2,1,0:T(8,128)(2,1)S(1)}, bf16[1,256,768]{2,1,0:T(8,128)(2,1)}, u32[]{:S(2)}) copy-start(bf16[1,256,768]{2,1,0:T(8,128)(2,1)} %get-tuple-element.115) | copy-start | bytes 1179652
  632.0 75.2 %copy-start.141 = (f32[768]{0:T(1024)S(1)}, f32[768]{0:T(1024)}, u32[]{:S(2)}) copy-start(f32[768]{0:T(1024)} %param.21) | copy-start | bytes 9220
  632.0 75.2 %copy-start.145 = (f32[256]{0:T(256)S(1)}, f32[256]{0:T(256)}, u32[]{:S(2)}) copy-start(f32[256]{0:T(256)} %copy-done.144) | copy-start | bytes 3076
  707.2 52.6 %copy-start.44 = (f32[1,256,768]{2,1,0:T(8,128)S(1)}, f32[1,256,768]{2,1,0:T(8,128)}, u32[]{:S(2)}) copy-start(f32[1,256,768]{2,1,0:T(8,128)} %copy-done.43) | copy-start | bytes 2359300
  707.2 52.7 %copy-start.150 = (f32[256]{0:T(256)S(1)}, f32[256]{0:T(256)}, u32[]{:S(2)}) copy-start(f32[256]{0:T(256)} %copy-done.149) | copy-start | bytes 3076
  707.2 52.6 %copy-start.117 = (bf16[1,256,768]{2,1,0:T(8,128)(2,1)S(1)}, bf16[1,256,768]{2,1,0:T(8,128)(2,1)}, u32[]{:S(2)}) copy-start(bf16[1,256,768]{2,1,0:T(8,128)(2,1)} %reduce-scatter.47.cloned.1.call-done) | copy-start | bytes 1179652
  (159 other events, 620.4 us)
Sparse Core Ops, SparseCore 0:
  38.1 31.3 reduce-scatter.24
  101.3 27.2 reduce-scatter.40
  131.3 17.4 reduce-scatter.26
  179.4 17.4 reduce-scatter.42
  227.4 29.7 reduce-scatter.28
  260.0 29.1 reduce-scatter.20
  292.0 37.1 reduce-scatter.16
  382.2 26.8 reduce-scatter.36
  411.4 26.0 reduce-scatter.44
  439.7 26.0 reduce-scatter.32
  468.6 17.4 reduce-scatter.18
  488.8 17.4 reduce-scatter.30
  509.1 23.6 reduce-scatter.22
  588.8 17.3 reduce-scatter.34
  609.3 17.3 reduce-scatter.38
  629.5 17.4 reduce-scatter.46
  653.1 261.7 all-reduce.4
where the time goes:
time: 940 us; the launch traced here: 932 us
  blocking collectives  307 us (33%)
  waiting for transfers between devices  255 us (27%)
  matrix products  229 us (24%)
  other arithmetic  87.3 us (9%)
  local copies, waits for them, and re-layouts  37.1 us (4%)
  between operations  16.6 us (2%)
    dot_general x96, matrix products, product(): jnp.einsum(pattern, left_side, right_side, preferred_element_type=jnp.flo...  229 us
    psum x1, waiting for transfers between devices, on_device(): lax.psum((sum_w_query, sum_b_query, sum_w_key, sum_w_value, sum_b_value,...  152 us
    all_gather x4, blocking collectives, on_device(): grad_full = lax.all_gather(upstream, 'mp', axis=1, tiled=True)  61.7 us
    psum x1, blocking collectives, on_device(): lax.psum((sum_w_query, sum_b_query, sum_w_key, sum_w_value, sum_b_value,...  60.4 us
    all_gather x4, blocking collectives, on_device(): lax.all_gather(normed_in.astype(jnp.bfloat16), 'mp', axis=1, tiled=True)  51.1 us
    reduce_scatter x4, waiting for transfers between devices, on_device(): lax.psum_scatter(product('bsf,fd->bsd', active, w_down).astype(jnp.bfloat...  51 us
    all_gather x4, blocking collectives, on_device(): lax.all_gather(grad_residual.astype(jnp.bfloat16), 'mp', axis=1, tiled=True)  48.7 us
    all_gather x4, blocking collectives, on_device(): lax.all_gather(normed_mid.astype(jnp.bfloat16), 'mp', axis=1, tiled=True)  45.3 us
  transfers between devices with their start and end apart: 17, of which 8 were waited for; matrix products, arithmetic and copies ran while one was open for 23% of the time, Pallas kernels for 0%

commit v1 on v0

--- a/solution.py
+++ b/solution.py
@@ -210,8 +210,10 @@
         )
     )
     common = lax.psum(
-        (sum_ln1_gain, sum_ln1_shift, sum_ln2_gain, sum_ln2_shift, sum_b_out, sum_b_down),
-        ("dp", "mp"),
+        lax.psum(
+            (sum_ln1_gain, sum_ln1_shift, sum_ln2_gain, sum_ln2_shift, sum_b_out, sum_b_down), "mp"
+        ),
+        "dp",
     )
     block_out = jnp.concatenate(outputs, axis=0)
     input_grad = jnp.concatenate(input_grads, axis=0)

time: 940 us -> 942 us (level)
  waiting for transfers between devices: 255 us -> 272 us
  blocking collectives: 307 us -> 293 us
    psum x1, blocking collectives: 39.4 us -> 8.35 us  [on_device(): lax.psum((sum_ln1_gain, sum_ln1_shift, sum_ln2_gain, sum_ln2_shift, sum_b...]
    psum x1, waiting for transfers between devices: 152 us -> 178 us  [on_device(): lax.psum((sum_w_query, sum_b_query, sum_w_key, sum_w_value, sum_b_value,...]
    all_gather x4, blocking collectives: 45.3 us -> 58.9 us  [on_device(): lax.all_gather(normed_mid.astype(jnp.bfloat16), 'mp', axis=1, tiled=True)]
    reduce_scatter x4, waiting for transfers between devices: 51 us -> 39.6 us  [on_device(): lax.psum_scatter(product('bsf,fd->bsd', active, w_down).astype(jnp.bfloat...]
    unnamed x418 -> x448, local copies, waits for them, and re-layouts: 31.2 us -> 31.5 us
  transfers between devices with their start and end apart: 17 -> 17, of which waited for: 8 -> 9; matrix products, arithmetic and copies ran while one was open for 23% -> 22% of each run, Pallas kernels for 0% -> 0%
where the time goes in v1:
time: 942 us; the launch traced here: 934 us
  blocking collectives  293 us (31%)
  waiting for transfers between devices  272 us (29%)
  matrix products  224 us (24%)
  other arithmetic  88.4 us (9%)
  local copies, waits for them, and re-layouts  37.3 us (4%)
  between operations  16.7 us (2%)
    dot_general x96, matrix products, product(): jnp.einsum(pattern, left_side, right_side, preferred_element_type=jnp.flo...  224 us
    psum x1, waiting for transfers between devices, on_device(): lax.psum((sum_w_query, sum_b_query, sum_w_key, sum_w_value, sum_b_value,...  178 us
    psum x1, blocking collectives, on_device(): lax.psum(lax.psum((sum_ln1_gain, sum_ln1_shift, sum_ln2_gain, sum_ln2_shi...  64.5 us
    all_gather x4, blocking collectives, on_device(): grad_full = lax.all_gather(upstream, 'mp', axis=1, tiled=True)  62.4 us
    all_gather x4, blocking collectives, on_device(): lax.all_gather(normed_mid.astype(jnp.bfloat16), 'mp', axis=1, tiled=True)  58.9 us
    all_gather x4, blocking collectives, on_device(): lax.all_gather(normed_in.astype(jnp.bfloat16), 'mp', axis=1, tiled=True)  50.9 us
    all_gather x4, blocking collectives, on_device(): lax.all_gather(grad_residual.astype(jnp.bfloat16), 'mp', axis=1, tiled=True)  48.2 us
    reduce_scatter x4, waiting for transfers between devices, on_device(): lax.psum_scatter(product('bsf,fd->bsd', active, w_down).astype(jnp.bfloat...  39.6 us
  transfers between devices with their start and end apart: 17, of which 9 were waited for; matrix products, arithmetic and copies ran while one was open for 22% of the time, Pallas kernels for 0%

profile of v1, /device:TPU:0, one launch (start us, length us, event | category | flops | bytes accessed | tf_op | source)
XLA Modules:
  0.0 934.0 jit_solution(2510134234578043178)
XLA Ops:
  12.2 12.8 %all_gather.52 = bf16[1,512,768]{2,1,0:T(8,128)(2,1)S(1)} all-gather(bf16[1,256,768]{2,1,0:T(8,128)(2,1)S(1)} %fusion.127), channel_id=1, replica_groups=mesh['dp'=16,'mp'=2] {'mp'}, dimensions={1}, use_global_device_ids=true | all-gather | bytes 1179648 | tf_op jit(solution)/shard_map/all_gather | solution.py:96
  38.0 2.4 fusion.226
  40.4 16.8 %all_gather.60 = bf16[1,512,768]{2,1,0:T(8,128)(2,1)} all-gather(bf16[1,256,768]{2,1,0:T(8,128)(2,1)S(1)} %get-tuple-element.119), channel_id=1, replica_groups=mesh['dp'=16,'mp'=2] {'mp'}, dimensions={1}, use_global_device_ids=true | all-gather | bytes 1179648 | tf_op jit(solution)/shard_map/all_gather | solution.py:138
  57.2 12.3 %reduce-scatter.25.cloned.1.call-done = f32[1,256,768]{2,1,0:T(8,128)} async-done(((f32[1,512,768]{2,1,0:T(8,128)}), f32[1,256,768]{2,1,0:T(8,128)}) %reduce-scatter.25.cloned.1.call-update) | async-done | bytes 786448 | tf_op jit(solution)/shard_map/reduce_scatter | solution.py:123
  72.1 12.1 %all_gather.53 = bf16[1,512,768]{2,1,0:T(8,128)(2,1)S(1)} all-gather(bf16[1,256,768]{2,1,0:T(8,128)(2,1)S(1)} %add_convert_fusion.7), channel_id=1, replica_groups=mesh['dp'=16,'mp'=2] {'mp'}, dimensions={1}, use_global_device_ids=true | all-gather | bytes 1179648 | tf_op jit(solution)/shard_map/all_gather | solution.py:128
  84.1 10.3 %fusion.16 = (bf16[512,1536]{1,0:T(8,128)(2,1)}, f32[512,1536]{1,0:T(8,128)S(1)}) fusion(f32[1536]{0:T(1024)} %param.33, bf16[768,1536]{1,0:T(8,128)(2,1)S(1)} %copy-done, bf16[1,512,768]{2,1,0:T(8,128)(2,1)S(1)} %all_gather.53), kind=kOutput, calls=%fused_computation.54 | convolution fusion | flops 1259864064 | bytes 7870464 | tf_op jit(solution)/shard_map/bsd,df->bsf/dot_general | solution.py:38
  94.4 2.8 convert_reduce_fusion.1
  98.4 2.6 convolution_bitcast_fusion.5
  101.0 4.4 fusion.70
  105.5 22.8 %reduce-scatter.41.cloned.1.call-done = f32[1,256,768]{2,1,0:T(8,128)} async-done(((f32[1,512,768]{2,1,0:T(8,128)}), f32[1,256,768]{2,1,0:T(8,128)}) %reduce-scatter.41.cloned.1.call-update) | async-done | bytes 786448 | tf_op jit(solution)/shard_map/reduce_scatter | solution.py:147
  131.1 17.6 %reduce-scatter.27.cloned.1.call-done = bf16[1,256,768]{2,1,0:T(8,128)(2,1)} async-done(((bf16[1,512,768]{2,1,0:T(8,128)(2,1)}), bf16[1,256,768]{2,1,0:T(8,128)(2,1)}) %reduce-scatter.27.cloned.1.call-update) | async-done | bytes 393232 | tf_op jit(solution)/shard_map/reduce_scatter | solution.py:131
  148.7 3.6 convert_reduce_fusion.14
  152.3 12.0 %all_gather.61 = bf16[1,512,768]{2,1,0:T(8,128)(2,1)S(1)} all-gather(bf16[1,256,768]{2,1,0:T(8,128)(2,1)S(1)} %convert_element_type.620), channel_id=1, replica_groups=mesh['dp'=16,'mp'=2] {'mp'}, dimensions={1}, use_global_device_ids=true | all-gather | bytes 1179648 | tf_op jit(solution)/shard_map/all_gather | solution.py:154
  167.0 4.6 multiply_reduce_fusion.1
  181.1 15.5 %reduce-scatter.43.cloned.1.call-done = bf16[1,256,768]{2,1,0:T(8,128)(2,1)} async-done(((bf16[1,512,768]{2,1,0:T(8,128)(2,1)}), bf16[1,256,768]{2,1,0:T(8,128)(2,1)}) %reduce-scatter.43.cloned.1.call-update) | async-done | bytes 393232 | tf_op jit(solution)/shard_map/reduce_scatter | solution.py:190
  196.6 2.9 fusion.154
  199.6 2.6 fusion.139
  202.2 12.2 %all_gather.48 = bf16[1,512,768]{2,1,0:T(8,128)(2,1)S(1)} all-gather(bf16[1,256,768]{2,1,0:T(8,128)(2,1)S(1)} %get-tuple-element.101), channel_id=1, replica_groups=mesh['dp'=16,'mp'=2] {'mp'}, dimensions={1}, use_global_device_ids=true | all-gather | bytes 1179648 | tf_op jit(solution)/shard_map/all_gather | solution.py:96
  227.9 16.6 %all_gather.50 = bf16[1,512,768]{2,1,0:T(8,128)(2,1)S(1)} all-gather(bf16[1,256,768]{2,1,0:T(8,128)(2,1)} %get-tuple-element.102), channel_id=1, replica_groups=mesh['dp'=16,'mp'=2] {'mp'}, dimensions={1}, use_global_device_ids=true | all-gather | bytes 1179648 | tf_op jit(solution)/shard_map/all_gather | solution.py:96
  259.2 9.3 all_gather.54
  282.7 10.8 %all_gather.56 = bf16[1,512,768]{2,1,0:T(8,128)(2,1)} all-gather(bf16[1,256,768]{2,1,0:T(8,128)(2,1)} %get-tuple-element.116), channel_id=1, replica_groups=mesh['dp'=16,'mp'=2] {'mp'}, dimensions={1}, use_global_device_ids=true | all-gather | bytes 1179648 | tf_op jit(solution)/shard_map/all_gather | solution.py:138
  293.5 18.9 %all_gather.62 = bf16[1,512,768]{2,1,0:T(8,128)(2,1)} all-gather(bf16[1,256,768]{2,1,0:T(8,128)(2,1)} %get-tuple-element.118), channel_id=1, replica_groups=mesh['dp'=16,'mp'=2] {'mp'}, dimensions={1}, use_global_device_ids=true | all-gather | bytes 1179648 | tf_op jit(solution)/shard_map/all_gather | solution.py:138
  312.4 15.9 %all_gather.58 = bf16[1,512,768]{2,1,0:T(8,128)(2,1)} all-gather(bf16[1,256,768]{2,1,0:T(8,128)(2,1)S(1)} %copy-done.121), channel_id=1, replica_groups=mesh['dp'=16,'mp'=2] {'mp'}, dimensions={1}, use_global_device_ids=true | all-gather | bytes 1179648 | tf_op jit(solution)/shard_map/all_gather | solution.py:138
  328.7 2.3 fusion.218
  333.8 12.0 %all_gather.49 = bf16[1,512,768]{2,1,0:T(8,128)(2,1)S(1)} all-gather(bf16[1,256,768]{2,1,0:T(8,128)(2,1)S(1)} %get-tuple-element.124), channel_id=1, replica_groups=mesh['dp'=16,'mp'=2] {'mp'}, dimensions={1}, use_global_device_ids=true | all-gather | bytes 1179648 | tf_op jit(solution)/shard_map/all_gather | solution.py:128
  345.8 9.4 %fusion.10 = (bf16[512,1536]{1,0:T(8,128)(2,1)}, f32[512,1536]{1,0:T(8,128)S(1)}) fusion(f32[1536]{0:T(1024)S(1)} %copy-done.203, bf16[768,1536]{1,0:T(8,128)(2,1)S(1)} %copy-done, bf16[1,512,768]{2,1,0:T(8,128)(2,1)S(1)} %all_gather.49), kind=kOutput, calls=%fused_computation.48 | convolution fusion | flops 1259864064 | bytes 7870464 | tf_op jit(solution)/shard_map/bsd,df->bsf/dot_general | solution.py:38
  355.3 2.8 convert_reduce_fusion.3
  359.3 2.5 convolution_bitcast_fusion.7
  361.9 15.7 %all_gather.55 = bf16[1,512,768]{2,1,0:T(8,128)(2,1)S(1)} all-gather(bf16[1,256,768]{2,1,0:T(8,128)(2,1)} %get-tuple-element.126), channel_id=1, replica_groups=mesh['dp'=16,'mp'=2] {'mp'}, dimensions={1}, use_global_device_ids=true | all-gather | bytes 1179648 | tf_op jit(solution)/shard_map/all_gather | solution.py:128
  377.6 19.1 %all_gather.51 = bf16[1,512,768]{2,1,0:T(8,128)(2,1)} all-gather(bf16[1,256,768]{2,1,0:T(8,128)(2,1)S(1)} %get-tuple-element.125), channel_id=1, replica_groups=mesh['dp'=16,'mp'=2] {'mp'}, dimensions={1}, use_global_device_ids=true | all-gather | bytes 1179648 | tf_op jit(solution)/shard_map/all_gather | solution.py:128
  396.7 10.3 %fusion.19 = (bf16[512,1536]{1,0:T(8,128)(2,1)}, f32[512,1536]{1,0:T(8,128)S(1)}) fusion(f32[1536]{0:T(1024)} %param.33, bf16[768,1536]{1,0:T(8,128)(2,1)S(1)} %copy-done, bf16[1,512,768]{2,1,0:T(8,128)(2,1)S(1)} %all_gather.55), kind=kOutput, calls=%fused_computation.57 | convolution fusion | flops 1259864064 | bytes 7870464 | tf_op jit(solution)/shard_map/bsd,df->bsf/dot_general | solution.py:38
  407.0 2.8 convert_reduce_fusion
  411.0 2.6 convolution_bitcast_fusion.4
  414.1 9.8 %fusion.13 = (bf16[512,1536]{1,0:T(8,128)(2,1)}, f32[512,1536]{1,0:T(8,128)S(1)}) fusion(f32[1536]{0:T(1024)S(1)} %copy-done.204, bf16[768,1536]{1,0:T(8,128)(2,1)S(1)} %copy-done, bf16[1,512,768]{2,1,0:T(8,128)(2,1)} %all_gather.51), kind=kOutput, calls=%fused_computation.51 | convolution fusion | flops 1259864064 | bytes 7870464 | tf_op jit(solution)/shard_map/bsd,df->bsf/dot_general | solution.py:38
  423.9 2.8 convert_reduce_fusion.2
  427.9 2.6 convolution_bitcast_fusion.6
  430.6 4.4 fusion.71
  435.1 5.4 fusion.184
  440.5 3.6 fusion.162
  444.1 3.6 fusion.202
  450.3 5.4 fusion.193
  455.7 3.5 fusion.173
  459.2 3.7 fusion.167
  465.3 9.8 %add_add_fusion.1 = f32[768,1536]{1,0:T(8,128)} fusion(f32[768,1536]{1,0:T(8,128)} %fusion.184, f32[768,1536]{1,0:T(8,128)} %fusion.202, f32[768,1536]{1,0:T(8,128)} %fusion.193, bf16[512,1536]{1,0:T(8,128)(2,1)} %copy-done.129, bf16[1,512,768]{2,1,0:T(8,128)(2,1)} %copy-done.95), kind=kOutput, calls=%fused_computation.33 | convolution fusion | flops 1211498496 | bytes 21233664 | tf_op jit(solution)/shard_map/bsd,bsf->df/dot_general | solution.py:38
  475.2 9.2 add_add_fusion
  484.4 3.8 multiply_reduce_fusion.7
  490.0 20.2 %reduce-scatter.19.cloned.1.call-done = bf16[1,256,768]{2,1,0:T(8,128)(2,1)} async-done(((bf16[1,512,768]{2,1,0:T(8,128)(2,1)}), bf16[1,256,768]{2,1,0:T(8,128)(2,1)}) %reduce-scatter.19.cloned.1.call-update) | async-done | bytes 393232 | tf_op jit(solution)/shard_map/reduce_scatter | solution.py:131
  510.2 4.9 fusion.215
  515.2 19.0 %all_gather.63 = bf16[1,512,768]{2,1,0:T(8,128)(2,1)S(1)} all-gather(bf16[1,256,768]{2,1,0:T(8,128)(2,1)S(1)} %convert_element_type.637), channel_id=1, replica_groups=mesh['dp'=16,'mp'=2] {'mp'}, dimensions={1}, use_global_device_ids=true | all-gather | bytes 1179648 | tf_op jit(solution)/shard_map/all_gather | solution.py:154
  545.9 3.2 fusion.214
  549.2 8.5 all_gather.59
  558.2 4.6 multiply_reduce_fusion.2
  569.1 8.7 all_gather.57
  604.2 2.4 convolution_add_fusion.15
  608.3 2.4 convert_reduce_fusion.19
  610.7 3.7 fusion.72
  616.5 2.8 convolution_add_fusion.13
  641.8 2.6 pad_maximum_fusion.1
  646.3 3.0 reduce-scatter.35.cloned.1.call-done
  649.3 3.4 fusion.155
  655.3 8.4 all-reduce.2
  663.6 64.5 %all-reduce = (f32[768]{0:T(1024)}, f32[768]{0:T(1024)}, f32[384]{0:T(512)}, f32[384]{0:T(512)}, f32[768]{0:T(1024)}, /*index=5*/f32[768]{0:T(1024)}, f32[768]{0:T(1024)}, f32[1536]{0:T(1024)}, f32[768]{0:T(1024)}) all-reduce(f32[768]{0:T(1024)} %get-tuple-element.79, ...), channel_id=1, replica_groups=mesh['dp'=16,'mp'=2] {'dp'}, use_global_device_ids=true, to_apply=%region_65.66 | all-reduce | flops 6912 | bytes 55296 | tf_op jit(solution)/shard_map/psum | solution.py:212
  738.0 178.4 %all-reduce.5.cloned.1.call-done = (f32[768,384]{1,0:T(8,128)}, f32[768,384]{1,0:T(8,128)}, f32[768,384]{1,0:T(8,128)}, f32[384,768]{1,0:T(8,128)}, f32[768,1536]{1,0:T(8,128)}, /*index=5*/f32[1536,768]{1,0:T(8,128)}) async-done(((f32[768,384]{1,0:T(8,128)}, f32[768,384]{1,0:T(8,128)}, f32[768,384]{1,0:T(8,128)}, f32[384,768]{1,0:T(8,128)}, f32[768,1536]{1,0:T(8,128)}, /*index=5*/f32[1536,768]{1,0:T(8,128)}), ...) | async-done | bytes 14155792 | tf_op jit(solution)/shard_map/psum | solution.py:197
  916.4 2.5 copy.73
  (644 shorter events, 185.0 us)
Async XLA Ops:
  7.2 76.9 %copy-start = (bf16[768,1536]{1,0:T(8,128)(2,1)S(1)}, bf16[768,1536]{1,0:T(8,128)(2,1)}, u32[]{:S(2)}) copy-start(bf16[768,1536]{1,0:T(8,128)(2,1)} %param.32) | copy-start | bytes 7077892
  7.2 17.7 %copy-start.193 = (s32[4]{0:T(128)S(1)}, s32[4]{0:T(128)}, u32[]{:S(2)}) copy-start(s32[4]{0:T(128)} %param.19) | copy-start | bytes 52
  7.2 19.1 %copy-start.37 = (bf16[768,384]{1,0:T(8,128)(2,1)S(1)}, bf16[768,384]{1,0:T(8,128)(2,1)}, u32[]{:S(2)}) copy-start(bf16[768,384]{1,0:T(8,128)(2,1)} %param.25) | copy-start | bytes 1769476
  7.2 19.6 %copy-start.34 = (bf16[768,384]{1,0:T(8,128)(2,1)S(1)}, bf16[768,384]{1,0:T(8,128)(2,1)}, u32[]{:S(2)}) copy-start(bf16[768,384]{1,0:T(8,128)(2,1)} %param.23) | copy-start | bytes 1769476
  7.2 19.6 %copy-start.205 = (f32[384]{0:T(512)S(1)}, f32[384]{0:T(512)}, u32[]{:S(2)}) copy-start(f32[384]{0:T(512)} %param.24) | copy-start | bytes 4612
  7.2 62.2 %reduce-scatter.25.cloned.1.call-start = ((), (), s32[]{:S(2)}) async-start(), calls=%async_computation.20 | async-start | bytes 2359296 | tf_op jit(solution)/shard_map/reduce_scatter | solution.py:123
  8.6 18.8 %copy-start.158 = (f32[256]{0:T(256)}, f32[256]{0:T(256)S(1)}, u32[]{:S(2)}) copy-start(f32[256]{0:T(256)S(1)} %broadcast_multiply_fusion.19) | copy-start | bytes 3076
  10.9 18.1 %copy-start.175 = (f32[256]{0:T(256)}, f32[256]{0:T(256)S(1)}, u32[]{:S(2)}) copy-start(f32[256]{0:T(256)S(1)} %add_rsqrt_fusion.3) | copy-start | bytes 3076
  37.9 90.4 %reduce-scatter.41.cloned.1.call-start = ((), (), s32[]{:S(2)}) async-start(), calls=%async_computation.28 | async-start | bytes 2359296 | tf_op jit(solution)/shard_map/reduce_scatter | solution.py:147
  101.0 47.7 %reduce-scatter.27.cloned.1.call-start = ((), (), s32[]{:S(2)}) async-start(), calls=%async_computation.21 | async-start | bytes 1179648 | tf_op jit(solution)/shard_map/reduce_scatter | solution.py:131
  105.5 91.1 %reduce-scatter.43.cloned.1.call-start = ((), (), s32[]{:S(2)}) async-start(), calls=%async_computation.29 | async-start | bytes 1179648 | tf_op jit(solution)/shard_map/reduce_scatter | solution.py:190
  148.7 15.6 %copy-start.30 = (bf16[384,768]{1,0:T(8,128)(2,1)S(1)}, bf16[384,768]{1,0:T(8,128)(2,1)}, u32[]{:S(2)}) copy-start(bf16[384,768]{1,0:T(8,128)(2,1)} %param.28) | copy-start | bytes 1769476
  152.3 12.6 %copy-start.42 = (f32[1,256,768]{2,1,0:T(8,128)}, f32[1,256,768]{2,1,0:T(8,128)S(1)}, u32[]{:S(2)}) copy-start(f32[1,256,768]{2,1,0:T(8,128)S(1)} %get-tuple-element.115) | copy-start | bytes 2359300
  152.3 13.0 %copy-start.13 = (bf16[6,512,512]{1,2,0:T(8,128)(2,1)S(1)}, bf16[6,512,512]{1,2,0:T(8,128)(2,1)}, u32[]{:S(2)}) copy-start(bf16[6,512,512]{1,2,0:T(8,128)(2,1)} %copy-done.12) | copy-start | bytes 9437188
  177.5 19.1 %copy-start.144 = (f32[768]{0:T(1024)S(1)}, f32[768]{0:T(1024)}, u32[]{:S(2)}) copy-start(f32[768]{0:T(1024)} %param.21) | copy-start | bytes 9220
  179.0 149.3 %reduce-scatter.17.cloned.1.call-start = ((), (), s32[]{:S(2)}) async-start(), calls=%async_computation.16 | async-start | bytes 2359296 | tf_op jit(solution)/shard_map/reduce_scatter | solution.py:123
  180.4 35.2 %copy-start.148 = (f32[256]{0:T(256)}, f32[256]{0:T(256)S(1)}, u32[]{:S(2)}) copy-start(f32[256]{0:T(256)S(1)} %broadcast_multiply_fusion.17) | copy-start | bytes 3076
  181.1 34.5 %copy-start.156 = (f32[256]{0:T(256)}, f32[256]{0:T(256)S(1)}, u32[]{:S(2)}) copy-start(f32[256]{0:T(256)S(1)} %get-tuple-element.187) | copy-start | bytes 3076
  181.1 34.5 %copy-start.157 = (f32[256]{0:T(256)}, f32[256]{0:T(256)S(1)}, u32[]{:S(2)}) copy-start(f32[256]{0:T(256)S(1)} %get-tuple-element.188) | copy-start | bytes 3076
  199.5 16.1 %copy-start.206 = (f32[384]{0:T(512)S(1)}, f32[384]{0:T(512)}, u32[]{:S(2)}) copy-start(f32[384]{0:T(512)} %param.24) | copy-start | bytes 4612
  199.5 16.7 %copy-start.176 = (f32[256]{0:T(256)}, f32[256]{0:T(256)S(1)}, u32[]{:S(2)}) copy-start(f32[256]{0:T(256)S(1)} %add_rsqrt_fusion.7) | copy-start | bytes 3076
  199.5 16.7 %copy-start.177 = (f32[256]{0:T(256)}, f32[256]{0:T(256)S(1)}, u32[]{:S(2)}) copy-start(f32[256]{0:T(256)S(1)} %add_rsqrt_fusion.5) | copy-start | bytes 3076
  199.6 16.6 %copy-start.178 = (f32[256]{0:T(256)}, f32[256]{0:T(256)S(1)}, u32[]{:S(2)}) copy-start(f32[256]{0:T(256)S(1)} %add_rsqrt_fusion.1) | copy-start | bytes 3076
  202.2 14.0 %copy-start.39 = (bf16[768,384]{1,0:T(8,128)(2,1)S(1)}, bf16[768,384]{1,0:T(8,128)(2,1)}, u32[]{:S(2)}) copy-start(bf16[768,384]{1,0:T(8,128)(2,1)} %param.25) | copy-start | bytes 1769476
  225.5 21.0 %copy-start.207 = (f32[384]{0:T(512)S(1)}, f32[384]{0:T(512)}, u32[]{:S(2)}) copy-start(f32[384]{0:T(512)} %param.24) | copy-start | bytes 4612
  227.2 101.1 %reduce-scatter.21.cloned.1.call-start = ((), (), s32[]{:S(2)}) async-start(), calls=%async_computation.18 | async-start | bytes 2359296 | tf_op jit(solution)/shard_map/reduce_scatter | solution.py:123
  227.9 23.8 %copy-start.187 = (pred[512]{0:T(512)(128)(4,1)}, pred[512]{0:T(512)(128)(4,1)S(1)}, u32[]{:S(2)}) copy-start(pred[512]{0:T(512)(128)(4,1)S(1)} %iota_compare_fusion.2) | copy-start | bytes 1540
  258.6 70.1 %reduce-scatter.29.cloned.1.call-start = ((), (), s32[]{:S(2)}) async-start(), calls=%async_computation.22 | async-start | bytes 2359296 | tf_op jit(solution)/shard_map/reduce_scatter | solution.py:123
  259.2 16.5 %copy-start.189 = (pred[512]{0:T(512)(128)(4,1)}, pred[512]{0:T(512)(128)(4,1)S(1)}, u32[]{:S(2)}) copy-start(pred[512]{0:T(512)(128)(4,1)S(1)} %iota_compare_fusion) | copy-start | bytes 1540
  280.8 31.6 %copy-start.121 = (bf16[1,256,768]{2,1,0:T(8,128)(2,1)S(1)}, bf16[1,256,768]{2,1,0:T(8,128)(2,1)}, u32[]{:S(2)}) copy-start(bf16[1,256,768]{2,1,0:T(8,128)(2,1)} %get-tuple-element.117) | copy-start | bytes 1179652
  282.6 46.1 %copy-start.174 = (f32[768]{0:T(1024)S(1)}, f32[768]{0:T(1024)}, u32[]{:S(2)}) copy-start(f32[768]{0:T(1024)} %param.29) | copy-start | bytes 9220
  282.6 201.7 %reduce-scatter.33.cloned.1.call-start = ((), (), s32[]{:S(2)}) async-start(), calls=%async_computation.24 | async-start | bytes 2359296 | tf_op jit(solution)/shard_map/reduce_scatter | solution.py:147
  331.0 14.7 %copy-start.14 = (f32[1,256,768]{2,1,0:T(8,128)}, f32[1,256,768]{2,1,0:T(8,128)S(1)}, u32[]{:S(2)}) copy-start(f32[1,256,768]{2,1,0:T(8,128)S(1)} %get-tuple-element.94) | copy-start | bytes 2359300
  331.1 14.7 %copy-start.15 = (f32[1,256,768]{2,1,0:T(8,128)}, f32[1,256,768]{2,1,0:T(8,128)S(1)}, u32[]{:S(2)}) copy-start(f32[1,256,768]{2,1,0:T(8,128)S(1)} %get-tuple-element.113) | copy-start | bytes 2359300
  331.4 14.4 %copy-start.203 = (f32[1536]{0:T(1024)S(1)}, f32[1536]{0:T(1024)}, u32[]{:S(2)}) copy-start(f32[1536]{0:T(1024)} %param.33) | copy-start | bytes 18436
  361.8 122.5 %reduce-scatter.45.cloned.1.call-start = ((), (), s32[]{:S(2)}) async-start(), calls=%async_computation.30 | async-start | bytes 2359296 | tf_op jit(solution)/shard_map/reduce_scatter | solution.py:147
  377.6 29.4 %copy-start.95 = (bf16[1,512,768]{2,1,0:T(8,128)(2,1)}, bf16[1,512,768]{2,1,0:T(8,128)(2,1)S(1)}, u32[]{:S(2)}) copy-start(bf16[1,512,768]{2,1,0:T(8,128)(2,1)S(1)} %all_gather.55) | copy-start | bytes 2359300
  413.6 70.8 %reduce-scatter.37.cloned.1.call-start = ((), (), s32[]{:S(2)}) async-start(), calls=%async_computation.26 | async-start | bytes 2359296 | tf_op jit(solution)/shard_map/reduce_scatter | solution.py:147
  430.5 59.5 %reduce-scatter.31.cloned.1.call-start = ((), (), s32[]{:S(2)}) async-start(), calls=%async_computation.23 | async-start | bytes 1179648 | tf_op jit(solution)/shard_map/reduce_scatter | solution.py:131
  435.0 75.2 %reduce-scatter.19.cloned.1.call-start = ((), (), s32[]{:S(2)}) async-start(), calls=%async_computation.17 | async-start | bytes 1179648 | tf_op jit(solution)/shard_map/reduce_scatter | solution.py:131
  450.0 95.9 %reduce-scatter.23.cloned.1.call-start = ((), (), s32[]{:S(2)}) async-start(), calls=%async_computation.19 | async-start | bytes 1179648 | tf_op jit(solution)/shard_map/reduce_scatter | solution.py:131
  465.2 181.1 %reduce-scatter.47.cloned.1.call-start = ((), (), s32[]{:S(2)}) async-start(), calls=%async_computation.31 | async-start | bytes 1179648 | tf_op jit(solution)/shard_map/reduce_scatter | solution.py:190
  484.3 25.9 %copy-start.146 = (f32[768]{0:T(1024)S(1)}, f32[768]{0:T(1024)}, u32[]{:S(2)}) copy-start(f32[768]{0:T(1024)} %param.35) | copy-start | bytes 9220
  510.2 24.0 %copy-start.32 = (bf16[384,768]{1,0:T(8,128)(2,1)S(1)}, bf16[384,768]{1,0:T(8,128)(2,1)}, u32[]{:S(2)}) copy-start(bf16[384,768]{1,0:T(8,128)(2,1)} %param.28) | copy-start | bytes 1769476
  510.2 26.2 %slice-start.4 = ((s8[6291456]{0:T(1024)(128)(4,1)}), s8[4194304]{0:T(1024)(128)(4,1)S(1)}, s32[]{:S(2)}) async-start(s8[6291456]{0:T(1024)(128)(4,1)} %bitcast.416), calls=%async_computation.37 | async-start | bytes 8388608
  515.2 21.3 %copy-start.48 = (f32[1,256,768]{2,1,0:T(8,128)}, f32[1,256,768]{2,1,0:T(8,128)S(1)}, u32[]{:S(2)}) copy-start(f32[1,256,768]{2,1,0:T(8,128)S(1)} %get-tuple-element.109) | copy-start | bytes 2359300
  515.2 19.6 %copy-start.11 = (bf16[6,512,512]{1,2,0:T(8,128)(2,1)S(1)}, bf16[6,512,512]{1,2,0:T(8,128)(2,1)}, u32[]{:S(2)}) copy-start(bf16[6,512,512]{1,2,0:T(8,128)(2,1)} %copy-done.10) | copy-start | bytes 9437188
  515.2 21.3 %slice-start.5 = ((s8[6291456]{0:T(1024)(128)(4,1)}), s8[2097152]{0:T(1024)(128)(4,1)S(1)}, s32[]{:S(2)}) async-start(s8[6291456]{0:T(1024)(128)(4,1)} %bitcast.416), calls=%async_computation.38 | async-start | bytes 4194304
  536.5 54.4 %copy-start.57 = (bf16[6,64,512]{2,1,0:T(8,128)(2,1)}, bf16[6,64,512]{2,1,0:T(8,128)(2,1)S(1)}, u32[]{:S(2)}) copy-start(bf16[6,64,512]{2,1,0:T(8,128)(2,1)S(1)} %get-tuple-element.172) | copy-start | bytes 1179652
  545.9 12.3 %copy-start.142 = (f32[6,512]{1,0:T(8,128)S(1)}, f32[6,512]{1,0:T(8,128)}, u32[]{:S(2)}) copy-start(f32[6,512]{1,0:T(8,128)} %copy-done.141) | copy-start | bytes 36868
  545.9 11.7 %copy-start.33 = (bf16[384,768]{1,0:T(8,128)(2,1)S(1)}, bf16[384,768]{1,0:T(8,128)(2,1)}, u32[]{:S(2)}) copy-start(bf16[384,768]{1,0:T(8,128)(2,1)} %param.28) | copy-start | bytes 1769476
  545.9 12.3 %copy-start.133 = (bf16[512,384]{0,1:T(8,128)(2,1)S(1)}, bf16[512,384]{0,1:T(8,128)(2,1)}, u32[]{:S(2)}) copy-start(bf16[512,384]{0,1:T(8,128)(2,1)} %copy-done.132) | copy-start | bytes 1179652
  545.9 12.3 %copy-start.188 = (pred[512]{0:T(512)(128)(4,1)S(1)}, pred[512]{0:T(512)(128)(4,1)}, u32[]{:S(2)}) copy-start(pred[512]{0:T(512)(128)(4,1)} %copy-done.187) | copy-start | bytes 1540
  549.1 13.6 %copy-start.44 = (f32[1,256,768]{2,1,0:T(8,128)}, f32[1,256,768]{2,1,0:T(8,128)S(1)}, u32[]{:S(2)}) copy-start(f32[1,256,768]{2,1,0:T(8,128)S(1)} %get-tuple-element.86) | copy-start | bytes 2359300
  565.2 13.5 %slice-start = ((s8[6291456]{0:T(1024)(128)(4,1)}), s8[4194304]{0:T(1024)(128)(4,1)S(1)}, s32[]{:S(2)}) async-start(s8[6291456]{0:T(1024)(128)(4,1)} %bitcast.412), calls=%async_computation.33 | async-start | bytes 8388608
  567.2 11.5 %copy-start.140 = (f32[6,512]{1,0:T(8,128)S(1)}, f32[6,512]{1,0:T(8,128)}, u32[]{:S(2)}) copy-start(f32[6,512]{1,0:T(8,128)} %copy-done.139) | copy-start | bytes 36868
  567.2 11.5 %copy-start.186 = (pred[512]{0:T(512)(128)(4,1)S(1)}, pred[512]{0:T(512)(128)(4,1)}, u32[]{:S(2)}) copy-start(pred[512]{0:T(512)(128)(4,1)} %iota_compare_fusion.3) | copy-start | bytes 1540
  592.5 53.8 %reduce-scatter.39.cloned.1.call-start = ((), (), s32[]{:S(2)}) async-start(), calls=%async_computation.27 | async-start | bytes 1179648 | tf_op jit(solution)/shard_map/reduce_scatter | solution.py:190
  610.7 38.6 %reduce-scatter.35.cloned.1.call-start = ((), (), s32[]{:S(2)}) async-start(), calls=%async_computation.25 | async-start | bytes 1179648 | tf_op jit(solution)/shard_map/reduce_scatter | solution.py:190
  624.0 292.5 %all-reduce.5.cloned.1.call-start = ((), (), s32[]{:S(2)}) async-start(), calls=%async_computation.32 | async-start | bytes 28311552 | tf_op jit(solution)/shard_map/psum | solution.py:197
  631.2 18.1 %copy-start.145 = (f32[768]{0:T(1024)S(1)}, f32[768]{0:T(1024)}, u32[]{:S(2)}) copy-start(f32[768]{0:T(1024)} %param.21) | copy-start | bytes 9220
  631.2 18.1 %copy-start.149 = (f32[256]{0:T(256)S(1)}, f32[256]{0:T(256)}, u32[]{:S(2)}) copy-start(f32[256]{0:T(256)} %copy-done.148) | copy-start | bytes 3076
  631.2 101.3 %copy-start.43 = (f32[1,256,768]{2,1,0:T(8,128)S(1)}, f32[1,256,768]{2,1,0:T(8,128)}, u32[]{:S(2)}) copy-start(f32[1,256,768]{2,1,0:T(8,128)} %copy-done.42) | copy-start | bytes 2359300
  646.3 88.5 %copy-start.122 = (bf16[1,256,768]{2,1,0:T(8,128)(2,1)S(1)}, bf16[1,256,768]{2,1,0:T(8,128)(2,1)}, u32[]{:S(2)}) copy-start(bf16[1,256,768]{2,1,0:T(8,128)(2,1)} %reduce-scatter.39.cloned.1.call-done) | copy-start | bytes 1179652
  (174 other events, 676.8 us)
Sparse Core Ops, SparseCore 0:
  38.1 31.3 reduce-scatter.24
  101.1 27.2 reduce-scatter.40
  131.2 17.4 reduce-scatter.26
  179.2 17.4 reduce-scatter.42
  227.3 29.6 reduce-scatter.16
  259.8 28.8 reduce-scatter.20
  291.0 37.6 reduce-scatter.28
  361.9 37.5 reduce-scatter.32
  413.7 27.7 reduce-scatter.44
  443.6 26.0 reduce-scatter.36
  472.5 17.4 reduce-scatter.30
  492.8 17.4 reduce-scatter.18
  513.0 23.4 reduce-scatter.22
  592.6 17.4 reduce-scatter.46
  612.2 17.4 reduce-scatter.38
  631.9 17.4 reduce-scatter.34
  655.4 260.9 all-reduce.4
